TPU v7x, 256 devices: a whole 4x4x8 slice. The times are simulated.
256 devices in a mesh: row: 16 (over x, z_hi), col: 16 (over y, z_lo, core).
Axes of the slice: x: 4, y: 4, z: 8 (z_hi: 4, z_lo: 2; z = z_hi * 2 + z_lo), core: 2. Of those that a mesh axis runs over, the one named last changes fastest.
Arguments:
- object_field: float32 [2, 6144, 6144], P(None, 'row', 'col'), may hold values from -6 to 6
- probe: float32 [2, 256, 256], replicated, may hold values from -5 to 5
- amplitudes: float32 [8192, 8192], P('row', 'col'), may hold values from 0.2 to 3
- offsets: int32 [32, 32, 2], P('row', 'col'), may hold values from 0 to 128, as said below
Outputs:
- updated_object: float32 [2, 6144, 6144], P(None, 'row', 'col')
Inputs may be any that keep to these rules, and one draw needn't show every extreme that they name: Both offsets of every scan position lie in 0 to 128, and each end of that range is taken in every draw.
All inputs are finite; a program needn't handle non-finite values.
Results may differ from a plain program's by a relative error of at most 0.0003.
Values sent between devices are 32-bit elements; how exact they have to be, the bound alone decides.
A program may use at most 64 MiB of HBM per device.

v0:
```python
import functools

import jax
import jax.numpy as jnp
import ml_dtypes
import numpy as np
from jax import lax
from jax.experimental import pallas as pl
from jax.experimental.pallas import tpu as pltpu
from jax.sharding import PartitionSpec as P

WIN = 256
HALF = 128
MARGIN = 96
PITCH = 192
TILE = 384
ROWS = TILE + 2 * MARGIN
COLS = 640
OWN = 128

step_size = 0.3
tv_weight = 0.2
tv_smooth = 0.1
amp_floor = 0.5

MESH = pl.DeviceIdType.MESH


def dft_tables():
    n = np.arange(HALF)
    whole = []
    for odd in (0, 1):
        k = 2 * np.arange(HALF) + odd
        angle = 2.0 * np.pi * ((k[:, None] * n[None, :]) % WIN) / WIN
        cosine = np.cos(angle) / 16.0
        sine = np.sin(angle) / 16.0
        left_form = np.block([[cosine, sine], [-sine, cosine]])
        whole += [left_form, left_form.T]
    high = [m.astype(ml_dtypes.bfloat16) for m in whole]
    low = [(m - h.astype(np.float64)).astype(ml_dtypes.bfloat16) for m, h in zip(whole, high)]
    return np.stack(high + low)


def parity_table():
    table = np.zeros((WIN, WIN), ml_dtypes.bfloat16)
    order = np.concatenate([np.arange(0, WIN, 2), np.arange(1, WIN, 2)])
    table[order, np.arange(WIN)] = 1.0
    return np.stack([table, table.T])


def split(x):
    high = x.astype(jnp.bfloat16)
    return high, (x - high.astype(jnp.float32)).astype(jnp.bfloat16)


def thirds(x):
    high = x.astype(jnp.bfloat16)
    return high, *split(x - high.astype(jnp.float32))


def dot(a, b):
    return jnp.dot(a, b, preferred_element_type=jnp.float32)


def cat(a, b, axis):
    return jnp.concatenate([a, b], axis=axis)


def left(tables, k, x):
    high, low = split(x)
    return dot(tables[k], high) + dot(tables[k], low) + dot(tables[k + 4], high)


def right(x, tables, k):
    high, low = split(x)
    return dot(high, tables[k]) + dot(low, tables[k]) + dot(high, tables[k + 4])


def fitted(spectrum, amp):
    re, im = spectrum[:, :HALF], spectrum[:, HALF:]
    magnitude = jnp.sqrt(re * re + im * im)
    keeping = 1.0 - amp / jnp.maximum(magnitude, amp_floor)
    return cat(re * keeping, im * keeping, 1)


def back_field(re, im, amp, tables):
    even = left(tables, 0, cat(re[:HALF] + re[HALF:], im[:HALF] + im[HALF:], 0))
    odd = left(tables, 2, cat(re[:HALF] - re[HALF:], im[:HALF] - im[HALF:], 0))
    re, im = cat(even[:HALF], odd[:HALF], 0), cat(even[HALF:], odd[HALF:], 0)
    even = cat(re[:, :HALF] + re[:, HALF:], im[:, :HALF] + im[:, HALF:], 1)
    odd = cat(re[:, :HALF] - re[:, HALF:], im[:, :HALF] - im[:, HALF:], 1)
    even = fitted(right(even, tables, 1), amp[:, :HALF])
    odd = fitted(right(odd, tables, 3), amp[:, HALF:])
    u, v = right(even, tables, 0), right(odd, tables, 2)
    p, m = u + v, u - v
    re, im = cat(p[:, :HALF], m[:, :HALF], 1), cat(p[:, HALF:], m[:, HALF:], 1)
    u = left(tables, 1, cat(re[:HALF], im[:HALF], 0))
    v = left(tables, 3, cat(re[HALF:], im[HALF:], 0))
    p, m = u + v, u - v
    return cat(p[:HALF], m[:HALF], 0), cat(p[HALF:], m[HALF:], 0)


def window(ext, canvas, probes, amps, tables, row_shift, col_shift, number):
    top, first = number // 2 * PITCH, number % 2 * HALF
    by_row = lax.broadcasted_iota(jnp.int32, (HALF, WIN), 0) >= row_shift
    by_col = lax.broadcasted_iota(jnp.int32, (HALF, WIN), 1) >= col_shift

    def rows_at(part, start):
        near = ext[part, start : start + HALF, first : first + WIN]
        far = ext[part, start : start + HALF, first + WIN : first + 2 * WIN]
        return jnp.where(by_col, near, far)

    def cells(part):
        upper = jnp.where(by_row, rows_at(part, top), rows_at(part, top + WIN))
        return cat(upper, rows_at(part, top + HALF), 0)

    re, im = cells(0), cells(1)
    probe_re, probe_im = probes[number, 0], probes[number, 1]
    back_re, back_im = back_field(
        probe_re * re - probe_im * im, probe_re * im + probe_im * re, amps[number], tables
    )
    grads = (probe_re * back_re + probe_im * back_im, probe_re * back_im - probe_im * back_re)
    for part, grad in enumerate(grads):
        upper, lower = grad[:HALF], grad[HALF:]
        for start, value in (
            (top, jnp.where(by_row, upper, 0.0)),
            (top + HALF, lower),
            (top + WIN, jnp.where(by_row, 0.0, upper)),
        ):
            canvas[part, start : start + HALF, first : first + WIN] += jnp.where(by_col, value, 0.0)
            canvas[part, start : start + HALF, first + WIN : first + 2 * WIN] += jnp.where(
                by_col, 0.0, value
            )


def rolled(x, shift, axis):
    amount = jnp.full(x.shape, shift, jnp.int32)
    for bit in range(8):
        x = jnp.where((amount & (1 << bit)) != 0, pltpu.roll(x, 1 << bit, axis), x)
    return x


def lane_part(depth):
    return lax.broadcasted_iota(jnp.int32, (depth, 128), 1) // 32


def turned(x, amount):
    amount %= 128
    return pltpu.roll(x, amount, 1) if amount else x


def pack(source, lane, skip, starts, depth, target):
    part_of = lane_part(depth)
    for part in range(2):
        groups = [source[part, s : s + depth, lane : lane + 128] for s in starts]
        for third in range(3):
            value = turned(groups[0], -32 * third - skip)
            for g in range(1, 4):
                value = jnp.where(part_of == g, turned(groups[g], 32 * (g - third) - skip), value)
            target[part, third * depth : (third + 1) * depth, :] = value


def unpack(source, skip, depth, part, g, keep):
    part_of = lane_part(depth)
    value = jnp.zeros((depth, 128), jnp.float32)
    for third in range(3):
        block = turned(source[part, third * depth : (third + 1) * depth, :], skip + 32 * (third - g))
        value = jnp.where(part_of == third + skip // 32, block, value)
    return jnp.where(keep, value, 0.0)


def tv_rows(ext, start, depth):
    high = depth + 16
    first = MARGIN + start - 8
    fields = [ext[part, pl.ds(first, high), :] for part in range(2)]
    down = [pltpu.roll(f, high - 1, 0) - f for f in fields]
    right_ = [pltpu.roll(f, COLS - 1, 1) - f for f in fields]
    total = down[0] * down[0] + right_[0] * right_[0] + (down[1] * down[1] + right_[1] * right_[1])
    inverse = lax.rsqrt(total + tv_smooth)
    out = []
    for part in range(2):
        flow_down = down[part] * inverse
        flow_right = right_[part] * inverse
        value = pltpu.roll(flow_down, 1, 0) - flow_down + pltpu.roll(flow_right, 1, 1) - flow_right
        out.append(value[8 : depth + 8, OWN : OWN + TILE])
    return out


BLOCKS = (slice(OWN, OWN + 128), slice(OWN + 128, OWN + 256), slice(OWN + 256, OWN + 384))
EDGE_ROWS = ((0, 96, 384, 480), 96)
MID_ROWS = ((192, 240, 288, 336), 48)
OWN_ROWS = ((96, 192, 288, 384), 96)
CORNER_ROWS = ((0, 48, 480, 528), 48)


def kernel(
    offsets, obj, probe, amplitudes, tables, parity, out,
    ext, canvas, probes, amps,
    own_send, own_recv, corner_send, corner_recv,
    grad_edge_send, grad_edge_recv, grad_mid_send, grad_mid_recv,
    rows_recv,
    halo_mid_send, halo_mid_recv, halo_edge_send, halo_edge_recv,
    last_edge_send, last_edge_recv, last_mid_send, last_mid_recv,
    last_rows_recv,
    send_sem, recv_sem,
):
    row, col = lax.axis_index("row"), lax.axis_index("col")
    rows, cols = lax.axis_size("row"), lax.axis_size("col")
    above, below = (lax.rem(row + rows - 1, rows), col), (lax.rem(row + 1, rows), col)
    before, after = (row, lax.rem(col + cols - 1, cols)), (row, lax.rem(col + 1, cols))
    has_above, has_below = row > 0, row < rows - 1
    has_before, has_after = col > 0, col < cols - 1

    barrier = pltpu.get_barrier_semaphore()
    for device in (above, below, before, after):
        pl.semaphore_signal(barrier, inc=1, device_id=device, device_id_type=MESH)
    pl.semaphore_wait(barrier, 4)

    count = [0]
    everything, waited = [], []

    def send(source, target, device):
        number = count[0]
        count[0] += 1
        copy = pltpu.make_async_remote_copy(
            src_ref=source, dst_ref=target, send_sem=send_sem.at[number], recv_sem=recv_sem.at[number],
            device_id=device, device_id_type=MESH,
        )
        copy.start()
        everything.append(copy)
        return copy

    def send_rows(source, target, low, high, low_to, high_to, depth, source_lane, target_lane, block):
        a = slice(source_lane + 128 * block, source_lane + 128 * block + 128)
        b = slice(target_lane + 128 * block, target_lane + 128 * block + 128)
        return [
            send(source.at[:, low : low + depth, a], target(0).at[:, low_to : low_to + depth, b], above),
            send(source.at[:, high : high + depth, a], target(1).at[:, high_to : high_to + depth, b], below),
        ]

    def send_cols(source, lanes, groups, depth, sends, recvs):
        pack(source, lanes[0][0], lanes[0][1], groups, depth, sends.at[0])
        first = send(sends.at[0], recvs.at[0], before)
        pack(source, lanes[1][0], lanes[1][1], groups, depth, sends.at[1])
        return [first, send(sends.at[1], recvs.at[1], after)]

    def arrived(copies):
        for copy in copies:
            copy.wait_recv()

    own_lanes = ((OWN, 0), (OWN + 256, 32))
    margin_lanes = ((0, 32), (OWN + TILE, 0))

    first_rows = [
        send_rows(obj, lambda _: ext, 0, TILE - MARGIN, MARGIN + TILE, 0, MARGIN, 0, OWN, block)
        for block in (0, 2)
    ]
    ext[:, MARGIN : MARGIN + TILE, OWN : OWN + TILE] = obj[...]
    first_cols = send_cols(ext, own_lanes, *OWN_ROWS, own_send, own_recv)
    first_rows.append(
        send_rows(obj, lambda _: ext, 0, TILE - MARGIN, MARGIN + TILE, 0, MARGIN, 0, OWN, 1)
    )

    shifts = []
    for number in range(4):
        i, j = number // 2, number % 2
        shifts.append((offsets[i, j, 0], offsets[i, j, 1] + 32 + 64 * j))
    for number in range(4):
        for part in range(2):
            probes[number, part] = rolled(
                rolled(probe[part], shifts[number][0], 0), shifts[number][1], 1
            )
        i, j = number // 2, number % 2
        pattern = amplitudes[i * WIN : (i + 1) * WIN, j * WIN : (j + 1) * WIN]
        pattern = sum(dot(piece, parity[0]) for piece in thirds(pattern))
        amps[number] = sum(dot(parity[1], piece) for piece in thirds(pattern))
    canvas[...] = jnp.zeros_like(canvas)

    def settle_rows(block):
        arrived(first_rows[(0, 2, 1)[block]])
        lanes = BLOCKS[block]
        for start, keep in ((0, has_above), (MARGIN + TILE, has_below)):
            halo = ext[:, start : start + MARGIN, lanes]
            ext[:, start : start + MARGIN, lanes] = jnp.where(keep, halo, 0.0)

    settle_rows(0)
    settle_rows(2)
    first_corners = send_cols(ext, own_lanes, *CORNER_ROWS, corner_send, corner_recv)
    settle_rows(1)

    def place_halo(recvs, groups, depth):
        for part in range(2):
            for g, start in enumerate(groups):
                ext[part, start : start + depth, OWN + TILE :] = unpack(
                    recvs.at[0], 0, depth, part, g, has_after
                )
                ext[part, start : start + depth, :OWN] = unpack(
                    recvs.at[1], 32, depth, part, g, has_before
                )

    arrived(first_cols)
    place_halo(own_recv, *OWN_ROWS)
    arrived(first_corners)
    place_halo(corner_recv, *CORNER_ROWS)

    def gradients():
        for number in range(4):
            window(ext, canvas, probes, amps, tables, *shifts[number], number)

    def add_cols(recvs, groups, depth):
        for part in range(2):
            for g, start in enumerate(groups):
                canvas[part, start : start + depth, BLOCKS[2]] += unpack(
                    recvs.at[0], 32, depth, part, g, has_after
                )
                canvas[part, start : start + depth, BLOCKS[0]] += unpack(
                    recvs.at[1], 0, depth, part, g, has_before
                )

    gradients()
    edge_cols = send_cols(canvas, margin_lanes, *EDGE_ROWS, grad_edge_send, grad_edge_recv)
    mid_cols = send_cols(canvas, margin_lanes, *MID_ROWS, grad_mid_send, grad_mid_recv)

    def add_tv(number, carry):
        start = pl.multiple_of(number * 48, 8)
        for part, value in enumerate(tv_rows(ext, start, 48)):
            canvas[part, pl.ds(MARGIN + start, 48), OWN : OWN + TILE] += tv_weight * value
        return carry

    lax.fori_loop(0, 8, add_tv, 0)

    def send_middle(block):
        return send_rows(
            canvas, lambda k: rows_recv.at[k], 0, 384, 0, 0, 192, OWN, 0, block
        )

    def taken_rows(block):
        lanes = BLOCKS[block]
        theirs = slice(128 * block, 128 * block + 128)
        for start, source, keep, halo in ((384, 0, has_below, 480), (0, 1, has_above, 0)):
            inner = 384 if start else 96
            for part in range(2):
                for first, gate in ((halo, None), (inner, keep)):
                    at = first - start
                    theirs_sum = jnp.where(keep, rows_recv[source, part, at : at + 96, theirs], 0.0)
                    total = canvas[part, first : first + 96, lanes] + theirs_sum
                    if gate is None:
                        total = jnp.where(keep, total, 0.0)
                    ext[part, first : first + 96, lanes] -= step_size * total

    row_sums = {1: send_middle(1)}
    arrived(edge_cols)
    add_cols(grad_edge_recv, *EDGE_ROWS)
    row_sums[0] = send_middle(0)
    row_sums[2] = send_middle(2)
    arrived(mid_cols)
    add_cols(grad_mid_recv, *MID_ROWS)
    ext[:, 192:384, OWN : OWN + TILE] -= step_size * canvas[:, 192:384, OWN : OWN + TILE]
    mid_halo = send_cols(ext, own_lanes, *MID_ROWS, halo_mid_send, halo_mid_recv)
    for block in (0, 2):
        arrived(row_sums[block])
        taken_rows(block)
    edge_halo = send_cols(ext, own_lanes, *EDGE_ROWS, halo_edge_send, halo_edge_recv)
    arrived(row_sums[1])
    taken_rows(1)
    for copies in (edge_cols, mid_cols, *row_sums.values()):
        for copy in copies:
            copy.wait_send()
            waited.append(copy)
    canvas[...] = jnp.zeros_like(canvas)
    arrived(mid_halo)
    place_halo(halo_mid_recv, *MID_ROWS)
    arrived(edge_halo)
    place_halo(halo_edge_recv, *EDGE_ROWS)

    gradients()

    def send_last(block):
        return send_rows(
            canvas, lambda k: last_rows_recv.at[k], 0, MARGIN + TILE, 0, 0, MARGIN, OWN, 0, block
        )

    edge_cols = send_cols(canvas, margin_lanes, *EDGE_ROWS, last_edge_send, last_edge_recv)
    mid_cols = send_cols(canvas, margin_lanes, *MID_ROWS, last_mid_send, last_mid_recv)
    last_rows = {1: send_last(1)}

    def start_out(number, carry):
        start = pl.multiple_of(number * 48, 8)
        here = pl.ds(MARGIN + start, 48)
        for part, value in enumerate(tv_rows(ext, start, 48)):
            out[part, pl.ds(start, 48), :] = (
                ext[part, here, OWN : OWN + TILE] - (step_size * tv_weight) * value
            )
        return carry

    lax.fori_loop(0, 8, start_out, 0)
    arrived(edge_cols)
    add_cols(last_edge_recv, *EDGE_ROWS)
    last_rows[0] = send_last(0)
    last_rows[2] = send_last(2)
    arrived(mid_cols)
    add_cols(last_mid_recv, *MID_ROWS)
    out[...] -= step_size * canvas[:, MARGIN : MARGIN + TILE, OWN : OWN + TILE]
    for block in (1, 0, 2):
        arrived(last_rows[block])
        lanes = slice(128 * block, 128 * block + 128)
        for start, source, keep in ((TILE - MARGIN, 0, has_below), (0, 1, has_above)):
            theirs = jnp.where(keep, last_rows_recv[source, :, :, lanes], 0.0)
            out[:, start : start + MARGIN, lanes] -= step_size * theirs
    for copy in everything:
        if not any(copy is other for other in waited):
            copy.wait_send()


def on_device(object_field, probe, amplitudes, offsets):
    vmem = pl.BlockSpec(memory_space=pltpu.VMEM)

    def pair(depth):
        return [pltpu.VMEM((2, 2, depth, 128), jnp.float32)] * 2

    return pl.pallas_call(
        kernel,
        out_shape=jax.ShapeDtypeStruct((2, TILE, TILE), jnp.float32),
        in_specs=[pl.BlockSpec(memory_space=pltpu.SMEM)] + [vmem] * 5,
        out_specs=vmem,
        scratch_shapes=[
            pltpu.VMEM((2, ROWS, COLS), jnp.float32),
            pltpu.VMEM((2, ROWS, COLS), jnp.float32),
            pltpu.VMEM((4, 2, WIN, WIN), jnp.float32),
            pltpu.VMEM((4, WIN, WIN), jnp.float32),
            *pair(288), *pair(144),
            *pair(288), *pair(144),
            pltpu.VMEM((2, 2, 192, TILE), jnp.float32),
            *pair(144), *pair(288),
            *pair(288), *pair(144),
            pltpu.VMEM((2, 2, MARGIN, TILE), jnp.float32),
            pltpu.SemaphoreType.DMA((34,)),
            pltpu.SemaphoreType.DMA((34,)),
        ],
        compiler_params=pltpu.CompilerParams(
            collective_id=0, has_side_effects=True, vmem_limit_bytes=56 << 20
        ),
        name="ptycho",
    )(offsets, object_field, probe, amplitudes, jnp.asarray(dft_tables()), jnp.asarray(parity_table()))


def solution(mesh):
    in_specs = (P(None, "row", "col"), P(), P("row", "col"), P("row", "col", None))
    out_specs = P(None, "row", "col")
    return jax.shard_map(
        on_device, mesh=mesh, in_specs=in_specs, out_specs=out_specs, check_vma=False
    )
```

profile of v0, /device:TPU:17, one launch (start us, length us, event | category | flops | bytes accessed | tf_op | source)
XLA Modules:
  0.0 122.9 jit_solution(217649134526888244)
XLA Ops:
  0.0 120.6 %ptycho.1 = f32[2,384,384]{2,1,0:T(8,128)} custom-call(s32[2,2,2]{2,1,0:T(2,128)} %offsets.1, f32[2,384,384]{2,1,0:T(8,128)} %obj.1, f32[2,256,256]{2,1,0:T(8,128)} %probe.1, f32[512,512]{1,0:T(8,128)} %amplitudes.1, bf16[8,256,256]{2,1,0:T(8,128)(2,1)} %constant.4.clone.tables, bf16[2,256,256]{2,1,0:T(8,128)(2,1)} %constant.5.clone.parity), custom_call_target="tpu_custom_call" | custom-call | tf_op jit(solution)/shard_map/ptycho/pallas_call | solution.py:421
  120.6 2.4 %copy.8 = f32[2,384,384]{2,1,0:T(8,128)} copy(f32[2,384,384]{2,1,0:T(8,128)} %ptycho.1) | data formatting | bytes 2359296
where the time goes:
time: 123 us
  Pallas kernels  121 us (98%)
  local copies, waits for them, and re-layouts  2.36 us (2%)
    pallas_call x1, Pallas kernels, on_device(): pl.pallas_call(kernel, out_shape=jax.ShapeDtypeStruct((2, TILE, TILE), jn...  121 us

commit v1 on v0

--- a/solution.py
+++ b/solution.py
@@ -238,28 +238,53 @@
             send(source.at[:, high : high + depth, a], target(1).at[:, high_to : high_to + depth, b], below),
         ]
 
-    def send_cols(source, lanes, groups, depth, sends, recvs):
-        pack(source, lanes[0][0], lanes[0][1], groups, depth, sends.at[0])
-        first = send(sends.at[0], recvs.at[0], before)
-        pack(source, lanes[1][0], lanes[1][1], groups, depth, sends.at[1])
-        return [first, send(sends.at[1], recvs.at[1], after)]
-
-    def arrived(copies):
-        for copy in copies:
-            copy.wait_recv()
-
     own_lanes = ((OWN, 0), (OWN + 256, 32))
     margin_lanes = ((0, 32), (OWN + TILE, 0))
 
-    first_rows = [
-        send_rows(obj, lambda _: ext, 0, TILE - MARGIN, MARGIN + TILE, 0, MARGIN, 0, OWN, block)
-        for block in (0, 2)
-    ]
+    def send_cols(way, source, lanes, groups, depth, sends, recvs):
+        pack(source, *lanes[way], groups, depth, sends.at[way])
+        return [send(sends.at[way], recvs.at[way], after if way else before)]
+
+    def arrived(*lists):
+        for copies in lists:
+            for copy in copies:
+                copy.wait_recv()
+
+    def place_halo(way, recvs, groups, depth):
+        for part in range(2):
+            for g, start in enumerate(groups):
+                if way:
+                    ext[part, start : start + depth, :OWN] = unpack(
+                        recvs.at[1], 32, depth, part, g, has_before
+                    )
+                else:
+                    ext[part, start : start + depth, OWN + TILE :] = unpack(
+                        recvs.at[0], 0, depth, part, g, has_after
+                    )
+
+    def add_cols(way, recvs, groups, depth):
+        for part in range(2):
+            for g, start in enumerate(groups):
+                if way:
+                    canvas[part, start : start + depth, BLOCKS[0]] += unpack(
+                        recvs.at[1], 0, depth, part, g, has_before
+                    )
+                else:
+                    canvas[part, start : start + depth, BLOCKS[2]] += unpack(
+                        recvs.at[0], 32, depth, part, g, has_after
+                    )
+
+    def send_obj(block):
+        return send_rows(obj, lambda _: ext, 0, TILE - MARGIN, MARGIN + TILE, 0, MARGIN, 0, OWN, block)
+
+    def gradients(j):
+        for i in range(2):
+            window(ext, canvas, probes, amps, tables, *shifts[2 * i + j], 2 * i + j)
+
+    obj_rows = {0: send_obj(0), 2: send_obj(2)}
     ext[:, MARGIN : MARGIN + TILE, OWN : OWN + TILE] = obj[...]
-    first_cols = send_cols(ext, own_lanes, *OWN_ROWS, own_send, own_recv)
-    first_rows.append(
-        send_rows(obj, lambda _: ext, 0, TILE - MARGIN, MARGIN + TILE, 0, MARGIN, 0, OWN, 1)
-    )
+    own_right = send_cols(1, ext, own_lanes, *OWN_ROWS, own_send, own_recv)
+    obj_rows[1] = send_obj(1)
 
     shifts = []
     for number in range(4):
@@ -277,49 +302,32 @@
     canvas[...] = jnp.zeros_like(canvas)
 
     def settle_rows(block):
-        arrived(first_rows[(0, 2, 1)[block]])
+        arrived(obj_rows[block])
         lanes = BLOCKS[block]
         for start, keep in ((0, has_above), (MARGIN + TILE, has_below)):
             halo = ext[:, start : start + MARGIN, lanes]
             ext[:, start : start + MARGIN, lanes] = jnp.where(keep, halo, 0.0)
 
+    settle_rows(2)
+    corner_right = send_cols(1, ext, own_lanes, *CORNER_ROWS, corner_send, corner_recv)
+    own_left = send_cols(0, ext, own_lanes, *OWN_ROWS, own_send, own_recv)
     settle_rows(0)
-    settle_rows(2)
-    first_corners = send_cols(ext, own_lanes, *CORNER_ROWS, corner_send, corner_recv)
+    corner_left = send_cols(0, ext, own_lanes, *CORNER_ROWS, corner_send, corner_recv)
     settle_rows(1)
-
-    def place_halo(recvs, groups, depth):
-        for part in range(2):
-            for g, start in enumerate(groups):
-                ext[part, start : start + depth, OWN + TILE :] = unpack(
-                    recvs.at[0], 0, depth, part, g, has_after
-                )
-                ext[part, start : start + depth, :OWN] = unpack(
-                    recvs.at[1], 32, depth, part, g, has_before
-                )
-
-    arrived(first_cols)
-    place_halo(own_recv, *OWN_ROWS)
-    arrived(first_corners)
-    place_halo(corner_recv, *CORNER_ROWS)
-
-    def gradients():
-        for number in range(4):
-            window(ext, canvas, probes, amps, tables, *shifts[number], number)
-
-    def add_cols(recvs, groups, depth):
-        for part in range(2):
-            for g, start in enumerate(groups):
-                canvas[part, start : start + depth, BLOCKS[2]] += unpack(
-                    recvs.at[0], 32, depth, part, g, has_after
-                )
-                canvas[part, start : start + depth, BLOCKS[0]] += unpack(
-                    recvs.at[1], 0, depth, part, g, has_before
-                )
-
-    gradients()
-    edge_cols = send_cols(canvas, margin_lanes, *EDGE_ROWS, grad_edge_send, grad_edge_recv)
-    mid_cols = send_cols(canvas, margin_lanes, *MID_ROWS, grad_mid_send, grad_mid_recv)
+    arrived(own_right)
+    place_halo(1, own_recv, *OWN_ROWS)
+    arrived(corner_right)
+    place_halo(1, corner_recv, *CORNER_ROWS)
+    gradients(0)
+    edge_left = send_cols(0, canvas, margin_lanes, *EDGE_ROWS, grad_edge_send, grad_edge_recv)
+    mid_left = send_cols(0, canvas, margin_lanes, *MID_ROWS, grad_mid_send, grad_mid_recv)
+    arrived(own_left)
+    place_halo(0, own_recv, *OWN_ROWS)
+    arrived(corner_left)
+    place_halo(0, corner_recv, *CORNER_ROWS)
+    gradients(1)
+    edge_right = send_cols(1, canvas, margin_lanes, *EDGE_ROWS, grad_edge_send, grad_edge_recv)
+    mid_right = send_cols(1, canvas, margin_lanes, *MID_ROWS, grad_mid_send, grad_mid_recv)
 
     def add_tv(number, carry):
         start = pl.multiple_of(number * 48, 8)
@@ -329,59 +337,79 @@
 
     lax.fori_loop(0, 8, add_tv, 0)
 
-    def send_middle(block):
-        return send_rows(
-            canvas, lambda k: rows_recv.at[k], 0, 384, 0, 0, 192, OWN, 0, block
-        )
-
-    def taken_rows(block):
-        lanes = BLOCKS[block]
+    def send_shared(block, part):
+        lanes = slice(128 * block, 128 * block + 128)
+        return [
+            send(canvas.at[part, :192, BLOCKS[block]], rows_recv.at[0, part, :, lanes], above),
+            send(canvas.at[part, 384:, BLOCKS[block]], rows_recv.at[1, part, :, lanes], below),
+        ]
+
+    def taken_rows(block, part):
         theirs = slice(128 * block, 128 * block + 128)
         for start, source, keep, halo in ((384, 0, has_below, 480), (0, 1, has_above, 0)):
             inner = 384 if start else 96
-            for part in range(2):
-                for first, gate in ((halo, None), (inner, keep)):
-                    at = first - start
-                    theirs_sum = jnp.where(keep, rows_recv[source, part, at : at + 96, theirs], 0.0)
-                    total = canvas[part, first : first + 96, lanes] + theirs_sum
-                    if gate is None:
-                        total = jnp.where(keep, total, 0.0)
-                    ext[part, first : first + 96, lanes] -= step_size * total
-
-    row_sums = {1: send_middle(1)}
-    arrived(edge_cols)
-    add_cols(grad_edge_recv, *EDGE_ROWS)
-    row_sums[0] = send_middle(0)
-    row_sums[2] = send_middle(2)
-    arrived(mid_cols)
-    add_cols(grad_mid_recv, *MID_ROWS)
+            for first in (halo, inner):
+                at = first - start
+                total = canvas[part, first : first + 96, BLOCKS[block]] + jnp.where(
+                    keep, rows_recv[source, part, at : at + 96, theirs], 0.0
+                )
+                if first == halo:
+                    total = jnp.where(keep, total, 0.0)
+                ext[part, first : first + 96, BLOCKS[block]] -= step_size * total
+
+    shared = {(1, 0): send_shared(1, 0)}
+    arrived(edge_left)
+    add_cols(0, grad_edge_recv, *EDGE_ROWS)
+    for part in range(2):
+        shared[2, part] = send_shared(2, part)
+    arrived(edge_right)
+    add_cols(1, grad_edge_recv, *EDGE_ROWS)
+    for part in range(2):
+        shared[0, part] = send_shared(0, part)
+    shared[1, 1] = send_shared(1, 1)
+    arrived(mid_left)
+    add_cols(0, grad_mid_recv, *MID_ROWS)
+    arrived(mid_right)
+    add_cols(1, grad_mid_recv, *MID_ROWS)
     ext[:, 192:384, OWN : OWN + TILE] -= step_size * canvas[:, 192:384, OWN : OWN + TILE]
-    mid_halo = send_cols(ext, own_lanes, *MID_ROWS, halo_mid_send, halo_mid_recv)
-    for block in (0, 2):
-        arrived(row_sums[block])
-        taken_rows(block)
-    edge_halo = send_cols(ext, own_lanes, *EDGE_ROWS, halo_edge_send, halo_edge_recv)
-    arrived(row_sums[1])
-    taken_rows(1)
-    for copies in (edge_cols, mid_cols, *row_sums.values()):
+    halo_mid_right = send_cols(1, ext, own_lanes, *MID_ROWS, halo_mid_send, halo_mid_recv)
+    for part in range(2):
+        arrived(shared[2, part])
+        taken_rows(2, part)
+    halo_edge_right = send_cols(1, ext, own_lanes, *EDGE_ROWS, halo_edge_send, halo_edge_recv)
+    halo_mid_left = send_cols(0, ext, own_lanes, *MID_ROWS, halo_mid_send, halo_mid_recv)
+    for part in range(2):
+        arrived(shared[0, part])
+        taken_rows(0, part)
+    halo_edge_left = send_cols(0, ext, own_lanes, *EDGE_ROWS, halo_edge_send, halo_edge_recv)
+    for part in range(2):
+        arrived(shared[1, part])
+        taken_rows(1, part)
+    for copies in shared.values():
         for copy in copies:
             copy.wait_send()
             waited.append(copy)
     canvas[...] = jnp.zeros_like(canvas)
-    arrived(mid_halo)
-    place_halo(halo_mid_recv, *MID_ROWS)
-    arrived(edge_halo)
-    place_halo(halo_edge_recv, *EDGE_ROWS)
-
-    gradients()
+    arrived(halo_mid_right)
+    place_halo(1, halo_mid_recv, *MID_ROWS)
+    arrived(halo_edge_right)
+    place_halo(1, halo_edge_recv, *EDGE_ROWS)
+    gradients(0)
+    edge_left = send_cols(0, canvas, margin_lanes, *EDGE_ROWS, last_edge_send, last_edge_recv)
+    mid_left = send_cols(0, canvas, margin_lanes, *MID_ROWS, last_mid_send, last_mid_recv)
+    arrived(halo_mid_left)
+    place_halo(0, halo_mid_recv, *MID_ROWS)
+    arrived(halo_edge_left)
+    place_halo(0, halo_edge_recv, *EDGE_ROWS)
+    gradients(1)
+    edge_right = send_cols(1, canvas, margin_lanes, *EDGE_ROWS, last_edge_send, last_edge_recv)
+    mid_right = send_cols(1, canvas, margin_lanes, *MID_ROWS, last_mid_send, last_mid_recv)
 
     def send_last(block):
         return send_rows(
             canvas, lambda k: last_rows_recv.at[k], 0, MARGIN + TILE, 0, 0, MARGIN, OWN, 0, block
         )
 
-    edge_cols = send_cols(canvas, margin_lanes, *EDGE_ROWS, last_edge_send, last_edge_recv)
-    mid_cols = send_cols(canvas, margin_lanes, *MID_ROWS, last_mid_send, last_mid_recv)
     last_rows = {1: send_last(1)}
 
     def start_out(number, carry):
@@ -394,14 +422,18 @@
         return carry
 
     lax.fori_loop(0, 8, start_out, 0)
-    arrived(edge_cols)
-    add_cols(last_edge_recv, *EDGE_ROWS)
+    arrived(edge_left)
+    add_cols(0, last_edge_recv, *EDGE_ROWS)
+    last_rows[2] = send_last(2)
+    arrived(edge_right)
+    add_cols(1, last_edge_recv, *EDGE_ROWS)
     last_rows[0] = send_last(0)
-    last_rows[2] = send_last(2)
-    arrived(mid_cols)
-    add_cols(last_mid_recv, *MID_ROWS)
+    arrived(mid_left)
+    add_cols(0, last_mid_recv, *MID_ROWS)
+    arrived(mid_right)
+    add_cols(1, last_mid_recv, *MID_ROWS)
     out[...] -= step_size * canvas[:, MARGIN : MARGIN + TILE, OWN : OWN + TILE]
-    for block in (1, 0, 2):
+    for block in (1, 2, 0):
         arrived(last_rows[block])
         lanes = slice(128 * block, 128 * block + 128)
         for start, source, keep in ((TILE - MARGIN, 0, has_below), (0, 1, has_above)):
@@ -434,8 +466,8 @@
             *pair(144), *pair(288),
             *pair(288), *pair(144),
             pltpu.VMEM((2, 2, MARGIN, TILE), jnp.float32),
-            pltpu.SemaphoreType.DMA((34,)),
-            pltpu.SemaphoreType.DMA((34,)),
+            pltpu.SemaphoreType.DMA((40,)),
+            pltpu.SemaphoreType.DMA((40,)),
         ],
         compiler_params=pltpu.CompilerParams(
             collective_id=0, has_side_effects=True, vmem_limit_bytes=56 << 20

time: 123 us -> 115 us (0.935)
  the two profiles are of different devices: /device:TPU:17 before, /device:TPU:2 now
where the time goes in v1:
time: 115 us; the launch traced here: 114 us
  Pallas kernels  111 us (97%)
  local copies, waits for them, and re-layouts  2.36 us (2%)
    pallas_call x1, Pallas kernels, on_device(): pl.pallas_call(kernel, out_shape=jax.ShapeDtypeStruct((2, TILE, TILE), jn...  111 us
    unnamed x1, local copies, waits for them, and re-layouts  2.36 us

profile of v1, /device:TPU:2, one launch (start us, length us, event | category | flops | bytes accessed | tf_op | source)
XLA Modules:
  0.0 113.8 jit_solution(15324721878558946089)
XLA Ops:
  0.0 111.4 %ptycho.1 = f32[2,384,384]{2,1,0:T(8,128)} custom-call(s32[2,2,2]{2,1,0:T(2,128)} %offsets.1, f32[2,384,384]{2,1,0:T(8,128)} %obj.1, f32[2,256,256]{2,1,0:T(8,128)} %probe.1, f32[512,512]{1,0:T(8,128)} %amplitudes.1, bf16[8,256,256]{2,1,0:T(8,128)(2,1)} %constant.4.clone.tables, bf16[2,256,256]{2,1,0:T(8,128)(2,1)} %constant.5.clone.parity), custom_call_target="tpu_custom_call" | custom-call | tf_op jit(solution)/shard_map/ptycho/pallas_call | solution.py:453
  111.4 2.4 %copy.8 = f32[2,384,384]{2,1,0:T(8,128)} copy(f32[2,384,384]{2,1,0:T(8,128)} %ptycho.1) | data formatting | bytes 2359296

commit v2 on v0

v2 whole, which is shorter than its diff:
```python
import functools

import jax
import jax.numpy as jnp
import ml_dtypes
import numpy as np
from jax import lax
from jax.experimental import pallas as pl
from jax.experimental.pallas import tpu as pltpu
from jax.sharding import PartitionSpec as P

WIN = 256
HALF = 128
MARGIN = 96
PITCH = 192
TILE = 384
ROWS = PITCH + 2 * MARGIN
COLS = 1024
OWN = 128
WIDE = 2 * TILE
BASES = (0, 128, 384, 512)

step_size = 0.3
tv_weight = 0.2
tv_smooth = 0.1
amp_floor = 0.5

MESH = pl.DeviceIdType.MESH


def dft_tables():
    n = np.arange(HALF)
    whole = []
    for odd in (0, 1):
        k = 2 * np.arange(HALF) + odd
        angle = 2.0 * np.pi * ((k[:, None] * n[None, :]) % WIN) / WIN
        cosine = np.cos(angle) / 16.0
        sine = np.sin(angle) / 16.0
        left_form = np.block([[cosine, sine], [-sine, cosine]])
        whole += [left_form, left_form.T]
    high = [m.astype(ml_dtypes.bfloat16) for m in whole]
    low = [(m - h.astype(np.float64)).astype(ml_dtypes.bfloat16) for m, h in zip(whole, high)]
    return np.stack(high + low)


def parity_table():
    table = np.zeros((WIN, WIN), ml_dtypes.bfloat16)
    order = np.concatenate([np.arange(0, WIN, 2), np.arange(1, WIN, 2)])
    table[order, np.arange(WIN)] = 1.0
    return np.stack([table, table.T])


def split(x):
    high = x.astype(jnp.bfloat16)
    return high, (x - high.astype(jnp.float32)).astype(jnp.bfloat16)


def thirds(x):
    high = x.astype(jnp.bfloat16)
    return high, *split(x - high.astype(jnp.float32))


def dot(a, b):
    return jnp.dot(a, b, preferred_element_type=jnp.float32)


def cat(a, b, axis):
    return jnp.concatenate([a, b], axis=axis)


def left(tables, k, x):
    high, low = split(x)
    return dot(tables[k], high) + dot(tables[k], low) + dot(tables[k + 4], high)


def right(x, tables, k):
    high, low = split(x)
    return dot(high, tables[k]) + dot(low, tables[k]) + dot(high, tables[k + 4])


def fitted(spectrum, amp):
    re, im = spectrum[:, :HALF], spectrum[:, HALF:]
    magnitude = jnp.sqrt(re * re + im * im)
    keeping = 1.0 - amp / jnp.maximum(magnitude, amp_floor)
    return cat(re * keeping, im * keeping, 1)


def back_field(re, im, amp, tables):
    even = left(tables, 0, cat(re[:HALF] + re[HALF:], im[:HALF] + im[HALF:], 0))
    odd = left(tables, 2, cat(re[:HALF] - re[HALF:], im[:HALF] - im[HALF:], 0))
    re, im = cat(even[:HALF], odd[:HALF], 0), cat(even[HALF:], odd[HALF:], 0)
    even = cat(re[:, :HALF] + re[:, HALF:], im[:, :HALF] + im[:, HALF:], 1)
    odd = cat(re[:, :HALF] - re[:, HALF:], im[:, :HALF] - im[:, HALF:], 1)
    even = fitted(right(even, tables, 1), amp[:, :HALF])
    odd = fitted(right(odd, tables, 3), amp[:, HALF:])
    u, v = right(even, tables, 0), right(odd, tables, 2)
    p, m = u + v, u - v
    re, im = cat(p[:, :HALF], m[:, :HALF], 1), cat(p[:, HALF:], m[:, HALF:], 1)
    u = left(tables, 1, cat(re[:HALF], im[:HALF], 0))
    v = left(tables, 3, cat(re[HALF:], im[HALF:], 0))
    p, m = u + v, u - v
    return cat(p[:HALF], m[:HALF], 0), cat(p[HALF:], m[HALF:], 0)


def spread(plane, shape):
    return jnp.broadcast_to(cat(plane[0:1, :], plane[0:1, :], 1), shape)


def window(ext, canvas, probes, amps, tables, shifts, number):
    first = BASES[number]
    shape = (HALF, WIN)
    by_row = lax.broadcasted_iota(jnp.int32, shape, 0) >= spread(shifts[number, 0], shape)
    by_col = lax.broadcasted_iota(jnp.int32, shape, 1) >= spread(shifts[number, 1], shape)

    def rows_at(part, start):
        near = ext[part, start : start + HALF, first : first + WIN]
        far = ext[part, start : start + HALF, first + WIN : first + 2 * WIN]
        return jnp.where(by_col, near, far)

    def cells(part):
        upper = jnp.where(by_row, rows_at(part, 0), rows_at(part, WIN))
        return cat(upper, rows_at(part, HALF), 0)

    re, im = cells(0), cells(1)
    probe_re, probe_im = probes[number, 0], probes[number, 1]
    back_re, back_im = back_field(
        probe_re * re - probe_im * im, probe_re * im + probe_im * re, amps[number], tables
    )
    grads = (probe_re * back_re + probe_im * back_im, probe_re * back_im - probe_im * back_re)
    for part, grad in enumerate(grads):
        upper, lower = grad[:HALF], grad[HALF:]
        for start, value in (
            (0, jnp.where(by_row, upper, 0.0)),
            (HALF, lower),
            (WIN, jnp.where(by_row, 0.0, upper)),
        ):
            canvas[part, start : start + HALF, first : first + WIN] += jnp.where(by_col, value, 0.0)
            canvas[part, start : start + HALF, first + WIN : first + 2 * WIN] += jnp.where(
                by_col, 0.0, value
            )


def rolled(x, amount, axis):
    for bit in range(8):
        x = jnp.where((amount & (1 << bit)) != 0, pltpu.roll(x, 1 << bit, axis), x)
    return x


def lane_part(depth):
    return lax.broadcasted_iota(jnp.int32, (depth, 128), 1) // 32


def turned(x, amount):
    amount %= 128
    return pltpu.roll(x, amount, 1) if amount else x


def pack(source, lane, skip, start, depth, target):
    part_of = lane_part(depth)
    for part in range(2):
        groups = [
            source[part, pl.ds(pl.multiple_of(start + g * depth, 8), depth), lane : lane + 128]
            for g in range(4)
        ]
        for third in range(3):
            value = turned(groups[0], -32 * third - skip)
            for g in range(1, 4):
                value = jnp.where(part_of == g, turned(groups[g], 32 * (g - third) - skip), value)
            target[part, third * depth : (third + 1) * depth, :] = value


def unpack(source, skip, depth, part, g, keep):
    part_of = lane_part(depth)
    value = jnp.zeros((depth, 128), jnp.float32)
    for third in range(3):
        block = turned(source[part, third * depth : (third + 1) * depth, :], skip + 32 * (third - g))
        value = jnp.where(part_of == third + skip // 32, block, value)
    return jnp.where(keep, value, 0.0)


def tv_rows(ext, start, depth):
    high = depth + 16
    first = pl.multiple_of(MARGIN + start - 8, 8)
    fields = [ext[part, pl.ds(first, high), :] for part in range(2)]
    down = [pltpu.roll(f, high - 1, 0) - f for f in fields]
    right_ = [pltpu.roll(f, COLS - 1, 1) - f for f in fields]
    total = down[0] * down[0] + right_[0] * right_[0] + (down[1] * down[1] + right_[1] * right_[1])
    inverse = lax.rsqrt(total + tv_smooth)
    out = []
    for part in range(2):
        flow_down = down[part] * inverse
        flow_right = right_[part] * inverse
        value = pltpu.roll(flow_down, 1, 0) - flow_down + pltpu.roll(flow_right, 1, 1) - flow_right
        out.append(value[8 : depth + 8, OWN : OWN + WIDE])
    return out


def lanes_of(block):
    return slice(OWN + 128 * block, OWN + 128 * block + 128)


def kernel(
    offsets, obj, probe_in, amplitudes, tables_in, parity_in, out,
    ext, canvas, canvas_2, probes, amps, probe, tables, parity,
    planes, shifts, raw_amps,
    first_send, first_recv, halo_send, halo_recv,
    grad_send, grad_recv, next_send, next_recv, last_send, last_recv,
    rows_recv, pair_recv, result, result_recv,
    send_sem, recv_sem, load_sem,
):
    row, col = lax.axis_index("row"), lax.axis_index("col")
    rows, cols = lax.axis_size("row"), lax.axis_size("col")
    quad, low, core = col // 4, lax.rem(col // 2, 2), lax.rem(col, 2)
    quads = cols // 4

    def device(at_row, at_quad, at_low, at_core):
        return (
            lax.rem(at_row + rows, rows),
            4 * lax.rem(at_quad + quads, quads) + 2 * at_low + at_core,
        )

    holder = [device(row, quad, core, k) for k in range(2)]
    holder_here = [(low == core) & (core == k) for k in range(2)]
    taker = [device(row, quad, k, low) for k in range(2)]
    taker_here = [(low == k) & (core == k) for k in range(2)]
    above = device(row - 1 + low, quad, 1 - low, core)
    below = device(row + low, quad, 1 - low, core)
    pair = device(row - 1 + 2 * low, quad, 1 - low, core)
    before = device(row, quad - 1 + core, low, 1 - core)
    after = device(row, quad + core, low, 1 - core)
    across = device(row, quad - 1 + 2 * core, low, 1 - core)
    has_above = (row > 0) | (low > 0)
    has_below = (row < rows - 1) | (low == 0)
    has_pair = ((low == 0) & (row > 0)) | ((low == 1) & (row < rows - 1))
    has_before = (quad > 0) | (core > 0)
    has_after = (quad < quads - 1) | (core == 0)

    loads = [
        pltpu.make_async_copy(source, target, load_sem.at[k])
        for k, (source, target) in enumerate(
            ((probe_in, probe), (parity_in, parity), (tables_in, tables))
        )
    ]
    for load in loads:
        load.start()
    barrier = pltpu.get_barrier_semaphore()
    for other in (
        device(row, quad, low, 1 - core), device(row, quad, 1 - low, core),
        device(row, quad, 1 - low, 1 - core), pair, across,
    ):
        pl.semaphore_signal(barrier, inc=1, device_id=other, device_id_type=MESH)
    pl.semaphore_wait(barrier, 5)

    sent, taken = [0], [0]
    ends = []

    def slots(count):
        taken[0] += count
        return taken[0] - count

    def send(source, target, other, slot, here=None):
        number = sent[0]
        sent[0] += 1
        remote = pltpu.make_async_remote_copy(
            src_ref=source, dst_ref=target, send_sem=send_sem.at[number], recv_sem=recv_sem.at[slot],
            device_id=other, device_id_type=MESH,
        )
        if here is None:
            remote.start()
            ends.append(remote.wait_send)
            return remote.wait_send
        local = pltpu.make_async_copy(source, target, recv_sem.at[slot])
        pl.when(here)(local.start)
        pl.when(jnp.logical_not(here))(remote.start)
        ends.append(lambda: pl.when(jnp.logical_not(here))(remote.wait_send))

    def arrived(target, slot):
        pltpu.make_async_copy(target, target, recv_sem.at[slot]).wait()

    def rows_from(start, depth):
        return pl.ds(pl.multiple_of(start, 8), depth)

    my_tile = pl.ds(pl.multiple_of(OWN + TILE * core, 128), TILE)

    def tile_lanes(k):
        return slice(OWN + TILE * k, OWN + TILE * k + TILE)

    for i in range(2):
        for j in range(2):
            planes[i, j, 0] = jnp.full((8, 128), offsets[i, j, 0], jnp.int32)
            planes[i, j, 1] = jnp.full((8, 128), offsets[i, j, 1] + (32 + 64 * j), jnp.int32)
    shift_slot, near_slot, far_slot = slots(2), slots(2), slots(2)
    two = pl.ds(2 * core, 2)
    for k in range(2):
        send(planes.at[k], shifts.at[two], taker[k], shift_slot + core, taker_here[k])
    for k, (start, to) in enumerate(((0, 96), (288, 192))):
        send(
            obj.at[:, start : start + 96, :], ext.at[:, to : to + 96, my_tile],
            taker[k], near_slot + core, taker_here[k],
        )
    for k, to in enumerate((192, 0)):
        send(
            obj.at[:, 96:288, :], ext.at[:, to : to + 192, my_tile],
            taker[k], far_slot + core, taker_here[k],
        )

    canvas[...] = jnp.zeros_like(canvas)
    canvas_2[...] = jnp.zeros_like(canvas_2)
    for k in range(2):
        arrived(shifts.at[2 * k : 2 * k + 2], shift_slot + k)

    edge = MARGIN + MARGIN * low
    halo = 288 * low
    pair_slot = slots(2)
    from_ext = []
    for k in range(2):
        arrived(ext.at[:, 0:96, tile_lanes(k)], near_slot + k)
        from_ext.append(
            send(
                ext.at[:, rows_from(edge, 96), tile_lanes(k)],
                ext.at[:, rows_from(288 - halo, 96), tile_lanes(k)], pair, pair_slot + k,
            )
        )
    amp_slot = slots(4)
    for j in range(2):
        for k in range(2):
            send(
                amplitudes.at[k * WIN : (k + 1) * WIN, j * WIN : (j + 1) * WIN],
                raw_amps.at[2 * core + j], taker[k], amp_slot + 2 * core + j, taker_here[k],
            )

    loads[0].wait()
    for number in range(4):
        for part in range(2):
            turn = [spread(shifts[number, axis], (WIN, WIN)) for axis in range(2)]
            probes[number, part] = rolled(rolled(probe[part], turn[0], 0), turn[1], 1)
    for load in loads[1:]:
        load.wait()

    own_lanes = ((OWN, 0), (OWN + WIDE - 128, 32))
    margin_lanes = ((0, 32), (OWN + WIDE, 0))

    def send_cols(way, source, lanes, start, depth, sends, recvs, slot):
        pack(source, *lanes[way], start, depth, sends.at[way])
        send(sends.at[way], recvs.at[way], after if way else before, slot + way)

    def place_halo(way, recvs, start, depth, slot):
        arrived(recvs.at[way], slot + way)
        for part in range(2):
            for g in range(4):
                here = rows_from(start + g * depth, depth)
                if way:
                    ext[part, here, :OWN] = unpack(recvs.at[1], 32, depth, part, g, has_before)
                else:
                    ext[part, here, OWN + WIDE :] = unpack(recvs.at[0], 0, depth, part, g, has_after)

    def add_cols(way, target, recvs, slot):
        arrived(recvs.at[way], slot + way)
        for part in range(2):
            for g in range(4):
                here = slice(96 * g, 96 * g + 96)
                if way:
                    target[part, here, lanes_of(0)] += unpack(recvs.at[1], 0, 96, part, g, has_before)
                else:
                    target[part, here, lanes_of(5)] += unpack(recvs.at[0], 32, 96, part, g, has_after)

    first_slot, halo_slot = slots(2), slots(2)
    most = MARGIN - MARGIN * low
    for k in range(2):
        arrived(ext.at[:, 0:192, tile_lanes(k)], far_slot + k)
    for way in (1, 0):
        send_cols(way, ext, own_lanes, most, 72, first_send, first_recv, first_slot)
    for k in range(2):
        arrived(ext.at[:, 0:96, tile_lanes(k)], pair_slot + k)
    here = rows_from(halo, 96)
    ext[:, here, OWN : OWN + WIDE] = jnp.where(has_pair, ext[:, here, OWN : OWN + WIDE], 0.0)
    for way in (1, 0):
        send_cols(way, ext, own_lanes, halo, 24, halo_send, halo_recv, halo_slot)

    def permuted(number):
        arrived(raw_amps.at[number], amp_slot + number)
        pattern = sum(dot(piece, parity[0]) for piece in thirds(raw_amps[number]))
        amps[number] = sum(dot(parity[1], piece) for piece in thirds(pattern))

    def gradient(target, number):
        window(ext, target, probes, amps, tables, shifts, number)

    def add_tv(number, carry):
        start = number * 48
        here = rows_from(MARGIN + start, 48)
        for part, value in enumerate(tv_rows(ext, start, 48)):
            canvas[part, here, OWN : OWN + WIDE] += tv_weight * value
        return carry

    row_slot = slots(12)

    def send_block(block):
        lanes = slice(128 * block, 128 * block + 128)
        slot = row_slot + 2 * block
        send(canvas.at[:, :192, lanes_of(block)], rows_recv.at[0, :, :, lanes], above, slot)
        send(canvas.at[:, 192:, lanes_of(block)], rows_recv.at[1, :, :, lanes], below, slot + 1)

    def take_block(block):
        theirs = slice(128 * block, 128 * block + 128)
        for source, keep, starts in ((1, has_above, (0, 96)), (0, has_below, (288, 192))):
            arrived(rows_recv.at[source, :, :, theirs], row_slot + 2 * block + source)
            for start in starts:
                at = start % 192
                for part in range(2):
                    total = canvas[part, start : start + 96, lanes_of(block)] + jnp.where(
                        keep, rows_recv[source, part, at : at + 96, theirs], 0.0
                    )
                    if start in (0, 288):
                        total = jnp.where(keep, total, 0.0)
                    ext[part, start : start + 96, lanes_of(block)] -= step_size * total

    place_halo(1, first_recv, most, 72, first_slot)
    place_halo(1, halo_recv, halo, 24, halo_slot)
    permuted(0)
    gradient(canvas, 0)
    grad_slot = slots(2)
    send_cols(0, canvas, margin_lanes, 0, 96, grad_send, grad_recv, grad_slot)
    permuted(1)
    gradient(canvas, 1)
    place_halo(0, first_recv, most, 72, first_slot)
    place_halo(0, halo_recv, halo, 24, halo_slot)
    lax.fori_loop(0, 4, add_tv, 0)
    send_block(1)
    permuted(2)
    gradient(canvas, 2)
    permuted(3)
    gradient(canvas, 3)
    send_cols(1, canvas, margin_lanes, 0, 96, grad_send, grad_recv, grad_slot)
    add_cols(0, canvas, grad_recv, grad_slot)
    send_block(5)
    send_block(2)
    add_cols(1, canvas, grad_recv, grad_slot)
    send_block(0)
    send_block(3)
    send_block(4)
    next_slot = slots(2)
    for end in from_ext:
        end()
        ends.remove(end)
    take_block(1)
    take_block(5)
    send_cols(1, ext, own_lanes, 0, 96, next_send, next_recv, next_slot)
    take_block(2)
    take_block(0)
    send_cols(0, ext, own_lanes, 0, 96, next_send, next_recv, next_slot)
    place_halo(1, next_recv, 0, 96, next_slot)
    gradient(canvas_2, 0)
    last_slot = slots(2)
    send_cols(0, canvas_2, margin_lanes, 0, 96, last_send, last_recv, last_slot)
    take_block(3)
    gradient(canvas_2, 1)
    take_block(4)
    gradient(canvas_2, 2)
    place_halo(0, next_recv, 0, 96, next_slot)
    gradient(canvas_2, 3)
    send_cols(1, canvas_2, margin_lanes, 0, 96, last_send, last_recv, last_slot)

    sum_slot, main_slot, rest_slot = slots(2), slots(4), slots(4)

    def send_pair(k):
        send(
            canvas_2.at[:, rows_from(halo, 96), tile_lanes(k)],
            pair_recv.at[:, :, TILE * k : TILE * k + TILE], pair, sum_slot + k,
        )

    def send_main(k):
        send(
            result.at[:, rows_from(192 - 192 * low, 192), TILE * k : TILE * k + TILE],
            result_recv.at[low], holder[k], main_slot + low, holder_here[k],
        )

    def finish(k):
        lanes = slice(TILE * k, TILE * k + TILE)
        result[:, :, lanes] -= step_size * canvas_2[:, :, tile_lanes(k)]

    def start_result(number, carry):
        start = number * 48
        here = rows_from(MARGIN + start, 48)
        for part, value in enumerate(tv_rows(ext, start, 48)):
            result[part, here, :] = ext[part, here, OWN : OWN + WIDE] - (step_size * tv_weight) * value
        return carry

    add_cols(0, canvas_2, last_recv, last_slot)
    send_pair(1)
    result[:, :MARGIN, :] = jnp.zeros((2, MARGIN, WIDE), jnp.float32)
    result[:, MARGIN + PITCH :, :] = jnp.zeros((2, MARGIN, WIDE), jnp.float32)
    lax.fori_loop(0, 4, start_result, 0)
    finish(1)
    send_main(1)
    add_cols(1, canvas_2, last_recv, last_slot)
    send_pair(0)
    finish(0)
    send_main(0)
    for k in (1, 0):
        lanes = slice(TILE * k, TILE * k + TILE)
        arrived(pair_recv.at[:, :, lanes], sum_slot + k)
        here = rows_from(edge, 96)
        result[:, here, lanes] -= jnp.where(has_pair, step_size * pair_recv[:, :, lanes], 0.0)
        send(
            result.at[:, here, lanes], out.at[:, rows_from(halo, 96), :],
            holder[k], rest_slot + low, holder_here[k],
        )
    for k in range(2):
        arrived(result_recv.at[k], main_slot + k)
    out[:, 96:288, :] = result_recv[0] + result_recv[1]
    for k, start in enumerate((0, 288)):
        arrived(out.at[:, start : start + 96, :], rest_slot + k)
    for end in ends:
        end()


def on_device(object_field, probe, amplitudes, offsets):
    vmem = pl.BlockSpec(memory_space=pltpu.VMEM)
    left_there = pl.BlockSpec(memory_space=pl.ANY)

    def pair(depth):
        return [pltpu.VMEM((2, 2, depth, 128), jnp.float32)] * 2

    tables, parity = dft_tables(), parity_table()
    return pl.pallas_call(
        kernel,
        out_shape=jax.ShapeDtypeStruct((2, TILE, TILE), jnp.float32),
        in_specs=[pl.BlockSpec(memory_space=pltpu.SMEM)] + [left_there] * 5,
        out_specs=vmem,
        scratch_shapes=[
            pltpu.VMEM((2, ROWS, COLS), jnp.float32),
            pltpu.VMEM((2, ROWS, COLS), jnp.float32),
            pltpu.VMEM((2, ROWS, COLS), jnp.float32),
            pltpu.VMEM((4, 2, WIN, WIN), jnp.float32),
            pltpu.VMEM((4, WIN, WIN), jnp.float32),
            pltpu.VMEM(probe.shape, jnp.float32),
            pltpu.VMEM(tables.shape, jnp.bfloat16),
            pltpu.VMEM(parity.shape, jnp.bfloat16),
            pltpu.VMEM((2, 2, 2, 8, 128), jnp.int32),
            pltpu.VMEM((4, 2, 8, 128), jnp.int32),
            pltpu.VMEM((4, WIN, WIN), jnp.float32),
            *pair(216), *pair(72),
            *pair(288), *pair(288), *pair(288),
            pltpu.VMEM((2, 2, 192, WIDE), jnp.float32),
            pltpu.VMEM((2, MARGIN, WIDE), jnp.float32),
            pltpu.VMEM((2, ROWS, WIDE), jnp.float32),
            pltpu.VMEM((2, 2, 192, TILE), jnp.float32),
            pltpu.SemaphoreType.DMA((64,)),
            pltpu.SemaphoreType.DMA((64,)),
            pltpu.SemaphoreType.DMA((3,)),
        ],
        compiler_params=pltpu.CompilerParams(
            collective_id=0, has_side_effects=True, vmem_limit_bytes=58 << 20
        ),
        name="ptycho",
    )(offsets, object_field, probe, amplitudes, jnp.asarray(tables), jnp.asarray(parity))


def solution(mesh):
    in_specs = (P(None, "row", "col"), P(), P("row", "col"), P("row", "col", None))
    out_specs = P(None, "row", "col")
    return jax.shard_map(
        on_device, mesh=mesh, in_specs=in_specs, out_specs=out_specs, check_vma=False
    )
```

time: 123 us -> 102 us (0.83)
  the two profiles are of different devices: /device:TPU:17 before, /device:TPU:2 now
where the time goes in v2:
time: 102 us
  Pallas kernels  100 us (98%)
  local copies, waits for them, and re-layouts  2.36 us (2%)
    pallas_call x1, Pallas kernels, on_device(): pl.pallas_call(kernel, out_shape=jax.ShapeDtypeStruct((2, TILE, TILE), jn...  100 us
    unnamed x1, local copies, waits for them, and re-layouts  2.36 us

profile of v2, /device:TPU:2, one launch (start us, length us, event | category | flops | bytes accessed | tf_op | source)
XLA Modules:
  0.0 102.3 jit_solution(1874891727850145005)
XLA Ops:
  0.0 100.0 %ptycho.1 = f32[2,384,384]{2,1,0:T(8,128)} custom-call(s32[2,2,2]{2,1,0:T(2,128)} %offsets.1, f32[2,384,384]{2,1,0:T(8,128)} %obj.1, f32[2,256,256]{2,1,0:T(8,128)} %probe_in.1, f32[512,512]{1,0:T(8,128)} %amplitudes.1, bf16[8,256,256]{2,1,0:T(8,128)(2,1)} %constant.4.clone.tables_in, bf16[2,256,256]{2,1,0:T(8,128)(2,1)} %constant.5.clone.parity_in), custom_call_target="tpu_custom_call" | custom-call | tf_op jit(solution)/shard_map/ptycho/pallas_call | solution.py:525
  100.0 2.4 %copy.8 = f32[2,384,384]{2,1,0:T(8,128)} copy(f32[2,384,384]{2,1,0:T(8,128)} %ptycho.1) | data formatting | bytes 2359296

commit v3 on v2

--- a/solution.py
+++ b/solution.py
@@ -18,6 +18,7 @@
 COLS = 1024
 OWN = 128
 WIDE = 2 * TILE
+HALF_LANES = TILE + 256
 BASES = (0, 128, 384, 512)
 
 step_size = 0.3
@@ -53,11 +54,6 @@
 def split(x):
     high = x.astype(jnp.bfloat16)
     return high, (x - high.astype(jnp.float32)).astype(jnp.bfloat16)
-
-
-def thirds(x):
-    high = x.astype(jnp.bfloat16)
-    return high, *split(x - high.astype(jnp.float32))
 
 
 def dot(a, b):
@@ -178,12 +174,13 @@
     return jnp.where(keep, value, 0.0)
 
 
-def tv_rows(ext, start, depth):
+def tv_rows(ext, start, depth, side):
     high = depth + 16
     first = pl.multiple_of(MARGIN + start - 8, 8)
-    fields = [ext[part, pl.ds(first, high), :] for part in range(2)]
+    lanes = slice(TILE * side, TILE * side + HALF_LANES)
+    fields = [ext[part, pl.ds(first, high), lanes] for part in range(2)]
     down = [pltpu.roll(f, high - 1, 0) - f for f in fields]
-    right_ = [pltpu.roll(f, COLS - 1, 1) - f for f in fields]
+    right_ = [pltpu.roll(f, HALF_LANES - 1, 1) - f for f in fields]
     total = down[0] * down[0] + right_[0] * right_[0] + (down[1] * down[1] + right_[1] * right_[1])
     inverse = lax.rsqrt(total + tv_smooth)
     out = []
@@ -191,7 +188,7 @@
         flow_down = down[part] * inverse
         flow_right = right_[part] * inverse
         value = pltpu.roll(flow_down, 1, 0) - flow_down + pltpu.roll(flow_right, 1, 1) - flow_right
-        out.append(value[8 : depth + 8, OWN : OWN + WIDE])
+        out.append(value[8 : depth + 8, OWN : OWN + TILE])
     return out
 
 
@@ -306,6 +303,8 @@
 
     canvas[...] = jnp.zeros_like(canvas)
     canvas_2[...] = jnp.zeros_like(canvas_2)
+    result[:, :MARGIN, :] = jnp.zeros((2, MARGIN, WIDE), jnp.float32)
+    result[:, MARGIN + PITCH :, :] = jnp.zeros((2, MARGIN, WIDE), jnp.float32)
     for k in range(2):
         arrived(shifts.at[2 * k : 2 * k + 2], shift_slot + k)
 
@@ -379,18 +378,21 @@
 
     def permuted(number):
         arrived(raw_amps.at[number], amp_slot + number)
-        pattern = sum(dot(piece, parity[0]) for piece in thirds(raw_amps[number]))
-        amps[number] = sum(dot(parity[1], piece) for piece in thirds(pattern))
+        pattern = sum(dot(piece, parity[0]) for piece in split(raw_amps[number]))
+        amps[number] = sum(dot(parity[1], piece) for piece in split(pattern))
 
     def gradient(target, number):
         window(ext, target, probes, amps, tables, shifts, number)
 
-    def add_tv(number, carry):
-        start = number * 48
-        here = rows_from(MARGIN + start, 48)
-        for part, value in enumerate(tv_rows(ext, start, 48)):
-            canvas[part, here, OWN : OWN + WIDE] += tv_weight * value
-        return carry
+    def add_tv(side):
+        def step(number, carry):
+            start = number * 48
+            here = rows_from(MARGIN + start, 48)
+            for part, value in enumerate(tv_rows(ext, start, 48, side)):
+                canvas[part, here, tile_lanes(side)] += tv_weight * value
+            return carry
+
+        lax.fori_loop(0, 4, step, 0)
 
     row_slot = slots(12)
 
@@ -414,9 +416,9 @@
                         total = jnp.where(keep, total, 0.0)
                     ext[part, start : start + 96, lanes_of(block)] -= step_size * total
 
+    permuted(0)
     place_halo(1, first_recv, most, 72, first_slot)
     place_halo(1, halo_recv, halo, 24, halo_slot)
-    permuted(0)
     gradient(canvas, 0)
     grad_slot = slots(2)
     send_cols(0, canvas, margin_lanes, 0, 96, grad_send, grad_recv, grad_slot)
@@ -424,16 +426,17 @@
     gradient(canvas, 1)
     place_halo(0, first_recv, most, 72, first_slot)
     place_halo(0, halo_recv, halo, 24, halo_slot)
-    lax.fori_loop(0, 4, add_tv, 0)
+    add_tv(0)
     send_block(1)
     permuted(2)
     gradient(canvas, 2)
+    send_block(2)
     permuted(3)
     gradient(canvas, 3)
     send_cols(1, canvas, margin_lanes, 0, 96, grad_send, grad_recv, grad_slot)
+    add_tv(1)
     add_cols(0, canvas, grad_recv, grad_slot)
     send_block(5)
-    send_block(2)
     add_cols(1, canvas, grad_recv, grad_slot)
     send_block(0)
     send_block(3)
@@ -443,73 +446,84 @@
         end()
         ends.remove(end)
     take_block(1)
+    take_block(2)
     take_block(5)
     send_cols(1, ext, own_lanes, 0, 96, next_send, next_recv, next_slot)
-    take_block(2)
     take_block(0)
     send_cols(0, ext, own_lanes, 0, 96, next_send, next_recv, next_slot)
     place_halo(1, next_recv, 0, 96, next_slot)
+
+    sum_slot, main_slot, rest_slot = slots(6), slots(6), slots(6)
+
+    def start_result(side):
+        def step(number, carry):
+            start = number * 48
+            here = rows_from(MARGIN + start, 48)
+            for part, value in enumerate(tv_rows(ext, start, 48, side)):
+                cells = ext[part, here, tile_lanes(side)]
+                result[part, here, TILE * side : TILE * side + TILE] = (
+                    cells - (step_size * tv_weight) * value
+                )
+            return carry
+
+        lax.fori_loop(0, 4, step, 0)
+
+    def finish(block):
+        lanes = slice(128 * block, 128 * block + 128)
+        there = slice(128 * (block % 3), 128 * (block % 3) + 128)
+        send(
+            canvas_2.at[:, rows_from(halo, 96), lanes_of(block)],
+            pair_recv.at[:, :, lanes], pair, sum_slot + block,
+        )
+        result[:, :, lanes] -= step_size * canvas_2[:, :, lanes_of(block)]
+        send(
+            result.at[:, rows_from(192 - 192 * low, 192), lanes], result_recv.at[low, :, :, there],
+            holder[block // 3], main_slot + 2 * (block % 3) + low, holder_here[block // 3],
+        )
+
+    def finish_rest(block):
+        lanes = slice(128 * block, 128 * block + 128)
+        there = slice(128 * (block % 3), 128 * (block % 3) + 128)
+        arrived(pair_recv.at[:, :, lanes], sum_slot + block)
+        here = rows_from(edge, 96)
+        result[:, here, lanes] -= jnp.where(has_pair, step_size * pair_recv[:, :, lanes], 0.0)
+        send(
+            result.at[:, here, lanes], out.at[:, rows_from(halo, 96), there],
+            holder[block // 3], rest_slot + 2 * (block % 3) + low, holder_here[block // 3],
+        )
+
     gradient(canvas_2, 0)
     last_slot = slots(2)
     send_cols(0, canvas_2, margin_lanes, 0, 96, last_send, last_recv, last_slot)
     take_block(3)
     gradient(canvas_2, 1)
+    start_result(0)
+    finish(1)
     take_block(4)
     gradient(canvas_2, 2)
+    finish(2)
     place_halo(0, next_recv, 0, 96, next_slot)
     gradient(canvas_2, 3)
     send_cols(1, canvas_2, margin_lanes, 0, 96, last_send, last_recv, last_slot)
-
-    sum_slot, main_slot, rest_slot = slots(2), slots(4), slots(4)
-
-    def send_pair(k):
-        send(
-            canvas_2.at[:, rows_from(halo, 96), tile_lanes(k)],
-            pair_recv.at[:, :, TILE * k : TILE * k + TILE], pair, sum_slot + k,
-        )
-
-    def send_main(k):
-        send(
-            result.at[:, rows_from(192 - 192 * low, 192), TILE * k : TILE * k + TILE],
-            result_recv.at[low], holder[k], main_slot + low, holder_here[k],
-        )
-
-    def finish(k):
-        lanes = slice(TILE * k, TILE * k + TILE)
-        result[:, :, lanes] -= step_size * canvas_2[:, :, tile_lanes(k)]
-
-    def start_result(number, carry):
-        start = number * 48
-        here = rows_from(MARGIN + start, 48)
-        for part, value in enumerate(tv_rows(ext, start, 48)):
-            result[part, here, :] = ext[part, here, OWN : OWN + WIDE] - (step_size * tv_weight) * value
-        return carry
-
+    finish_rest(1)
+    start_result(1)
+    finish(3)
+    finish(4)
     add_cols(0, canvas_2, last_recv, last_slot)
-    send_pair(1)
-    result[:, :MARGIN, :] = jnp.zeros((2, MARGIN, WIDE), jnp.float32)
-    result[:, MARGIN + PITCH :, :] = jnp.zeros((2, MARGIN, WIDE), jnp.float32)
-    lax.fori_loop(0, 4, start_result, 0)
-    finish(1)
-    send_main(1)
+    finish(5)
     add_cols(1, canvas_2, last_recv, last_slot)
-    send_pair(0)
     finish(0)
-    send_main(0)
-    for k in (1, 0):
-        lanes = slice(TILE * k, TILE * k + TILE)
-        arrived(pair_recv.at[:, :, lanes], sum_slot + k)
-        here = rows_from(edge, 96)
-        result[:, here, lanes] -= jnp.where(has_pair, step_size * pair_recv[:, :, lanes], 0.0)
-        send(
-            result.at[:, here, lanes], out.at[:, rows_from(halo, 96), :],
-            holder[k], rest_slot + low, holder_here[k],
-        )
-    for k in range(2):
-        arrived(result_recv.at[k], main_slot + k)
-    out[:, 96:288, :] = result_recv[0] + result_recv[1]
-    for k, start in enumerate((0, 288)):
-        arrived(out.at[:, start : start + 96, :], rest_slot + k)
+    for block in (2, 3, 4, 5, 0):
+        finish_rest(block)
+    for block in (1, 2, 0):
+        lanes = slice(128 * block, 128 * block + 128)
+        for k in range(2):
+            arrived(result_recv.at[k, :, :, lanes], main_slot + 2 * block + k)
+        out[:, 96:288, lanes] = result_recv[0, :, :, lanes] + result_recv[1, :, :, lanes]
+    for block in (1, 2, 0):
+        lanes = slice(128 * block, 128 * block + 128)
+        for k, start in enumerate((0, 288)):
+            arrived(out.at[:, start : start + 96, lanes], rest_slot + 2 * block + k)
     for end in ends:
         end()
 

time: 102 us -> 95.9 us (0.940)
  Pallas kernels: 100 us -> 93.3 us
    pallas_call x1, Pallas kernels: 100 us -> 93.3 us  [on_device(): pl.pallas_call(kernel, out_shape=jax.ShapeDtypeStruct((2, TILE, TILE), jn...]
where the time goes in v3:
time: 95.9 us; the launch traced here: 95.7 us
  Pallas kernels  93.3 us (97%)
  local copies, waits for them, and re-layouts  2.36 us (2%)
    pallas_call x1, Pallas kernels, on_device(): pl.pallas_call(kernel, out_shape=jax.ShapeDtypeStruct((2, TILE, TILE), jn...  93.3 us
    unnamed x1, local copies, waits for them, and re-layouts  2.36 us

profile of v3, /device:TPU:2, one launch (start us, length us, event | category | flops | bytes accessed | tf_op | source)
XLA Modules:
  0.0 95.7 jit_solution(5361152597987106781)
XLA Ops:
  0.0 93.3 %ptycho.1 = f32[2,384,384]{2,1,0:T(8,128)} custom-call(s32[2,2,2]{2,1,0:T(2,128)} %offsets.1, f32[2,384,384]{2,1,0:T(8,128)} %obj.1, f32[2,256,256]{2,1,0:T(8,128)} %probe_in.1, f32[512,512]{1,0:T(8,128)} %amplitudes.1, bf16[8,256,256]{2,1,0:T(8,128)(2,1)} %constant.4.clone.tables_in, bf16[2,256,256]{2,1,0:T(8,128)(2,1)} %constant.5.clone.parity_in), custom_call_target="tpu_custom_call" | custom-call | tf_op jit(solution)/shard_map/ptycho/pallas_call | solution.py:539
  93.3 2.4 %copy.8 = f32[2,384,384]{2,1,0:T(8,128)} copy(f32[2,384,384]{2,1,0:T(8,128)} %ptycho.1) | data formatting | bytes 2359296

commit v4 on v3

--- a/solution.py
+++ b/solution.py
@@ -18,7 +18,8 @@
 COLS = 1024
 OWN = 128
 WIDE = 2 * TILE
-HALF_LANES = TILE + 256
+THIRD = 256
+THIRD_LANES = THIRD + 256
 BASES = (0, 128, 384, 512)
 
 step_size = 0.3
@@ -177,10 +178,10 @@
 def tv_rows(ext, start, depth, side):
     high = depth + 16
     first = pl.multiple_of(MARGIN + start - 8, 8)
-    lanes = slice(TILE * side, TILE * side + HALF_LANES)
+    lanes = slice(THIRD * side, THIRD * side + THIRD_LANES)
     fields = [ext[part, pl.ds(first, high), lanes] for part in range(2)]
     down = [pltpu.roll(f, high - 1, 0) - f for f in fields]
-    right_ = [pltpu.roll(f, HALF_LANES - 1, 1) - f for f in fields]
+    right_ = [pltpu.roll(f, THIRD_LANES - 1, 1) - f for f in fields]
     total = down[0] * down[0] + right_[0] * right_[0] + (down[1] * down[1] + right_[1] * right_[1])
     inverse = lax.rsqrt(total + tv_smooth)
     out = []
@@ -188,7 +189,7 @@
         flow_down = down[part] * inverse
         flow_right = right_[part] * inverse
         value = pltpu.roll(flow_down, 1, 0) - flow_down + pltpu.roll(flow_right, 1, 1) - flow_right
-        out.append(value[8 : depth + 8, OWN : OWN + TILE])
+        out.append(value[8 : depth + 8, OWN : OWN + THIRD])
     return out
 
 
@@ -282,6 +283,9 @@
     def tile_lanes(k):
         return slice(OWN + TILE * k, OWN + TILE * k + TILE)
 
+    def third_lanes(side):
+        return slice(OWN + THIRD * side, OWN + THIRD * side + THIRD)
+
     for i in range(2):
         for j in range(2):
             planes[i, j, 0] = jnp.full((8, 128), offsets[i, j, 0], jnp.int32)
@@ -295,11 +299,15 @@
             obj.at[:, start : start + 96, :], ext.at[:, to : to + 96, my_tile],
             taker[k], near_slot + core, taker_here[k],
         )
-    for k, to in enumerate((192, 0)):
-        send(
-            obj.at[:, 96:288, :], ext.at[:, to : to + 192, my_tile],
-            taker[k], far_slot + core, taker_here[k],
-        )
+    inner_slot = slots(2)
+    for slot, lane, width in ((far_slot, 256 * core, 128), (inner_slot, 128 - 128 * core, 256)):
+        from_lanes = pl.ds(pl.multiple_of(lane, 128), width)
+        to_lanes = pl.ds(pl.multiple_of(OWN + TILE * core + lane, 128), width)
+        for k, to in enumerate((192, 0)):
+            send(
+                obj.at[:, 96:288, from_lanes], ext.at[:, to : to + 192, to_lanes],
+                taker[k], slot + core, taker_here[k],
+            )
 
     canvas[...] = jnp.zeros_like(canvas)
     canvas_2[...] = jnp.zeros_like(canvas_2)
@@ -366,7 +374,7 @@
     first_slot, halo_slot = slots(2), slots(2)
     most = MARGIN - MARGIN * low
     for k in range(2):
-        arrived(ext.at[:, 0:192, tile_lanes(k)], far_slot + k)
+        arrived(ext.at[:, 0:192, lanes_of(0)], far_slot + k)
     for way in (1, 0):
         send_cols(way, ext, own_lanes, most, 72, first_send, first_recv, first_slot)
     for k in range(2):
@@ -375,6 +383,8 @@
     ext[:, here, OWN : OWN + WIDE] = jnp.where(has_pair, ext[:, here, OWN : OWN + WIDE], 0.0)
     for way in (1, 0):
         send_cols(way, ext, own_lanes, halo, 24, halo_send, halo_recv, halo_slot)
+    for k in range(2):
+        arrived(ext.at[:, 0:192, 0:256], inner_slot + k)
 
     def permuted(number):
         arrived(raw_amps.at[number], amp_slot + number)
@@ -389,7 +399,7 @@
             start = number * 48
             here = rows_from(MARGIN + start, 48)
             for part, value in enumerate(tv_rows(ext, start, 48, side)):
-                canvas[part, here, tile_lanes(side)] += tv_weight * value
+                canvas[part, here, third_lanes(side)] += tv_weight * value
             return carry
 
         lax.fori_loop(0, 4, step, 0)
@@ -430,11 +440,12 @@
     send_block(1)
     permuted(2)
     gradient(canvas, 2)
+    add_tv(1)
     send_block(2)
     permuted(3)
     gradient(canvas, 3)
     send_cols(1, canvas, margin_lanes, 0, 96, grad_send, grad_recv, grad_slot)
-    add_tv(1)
+    add_tv(2)
     add_cols(0, canvas, grad_recv, grad_slot)
     send_block(5)
     add_cols(1, canvas, grad_recv, grad_slot)
@@ -460,8 +471,8 @@
             start = number * 48
             here = rows_from(MARGIN + start, 48)
             for part, value in enumerate(tv_rows(ext, start, 48, side)):
-                cells = ext[part, here, tile_lanes(side)]
-                result[part, here, TILE * side : TILE * side + TILE] = (
+                cells = ext[part, here, third_lanes(side)]
+                result[part, here, THIRD * side : THIRD * side + THIRD] = (
                     cells - (step_size * tv_weight) * value
                 )
             return carry
@@ -495,19 +506,20 @@
     gradient(canvas_2, 0)
     last_slot = slots(2)
     send_cols(0, canvas_2, margin_lanes, 0, 96, last_send, last_recv, last_slot)
+    start_result(0)
     take_block(3)
     gradient(canvas_2, 1)
-    start_result(0)
     finish(1)
     take_block(4)
     gradient(canvas_2, 2)
+    start_result(1)
     finish(2)
     place_halo(0, next_recv, 0, 96, next_slot)
     gradient(canvas_2, 3)
     send_cols(1, canvas_2, margin_lanes, 0, 96, last_send, last_recv, last_slot)
+    finish(3)
     finish_rest(1)
-    start_result(1)
-    finish(3)
+    start_result(2)
     finish(4)
     add_cols(0, canvas_2, last_recv, last_slot)
     finish(5)
@@ -515,21 +527,29 @@
     finish(0)
     for block in (2, 3, 4, 5, 0):
         finish_rest(block)
+    writes = []
     for block in (1, 2, 0):
         lanes = slice(128 * block, 128 * block + 128)
         for k in range(2):
             arrived(result_recv.at[k, :, :, lanes], main_slot + 2 * block + k)
-        out[:, 96:288, lanes] = result_recv[0, :, :, lanes] + result_recv[1, :, :, lanes]
+        result_recv[0, :, :, lanes] += result_recv[1, :, :, lanes]
+        writes.append(
+            pltpu.make_async_copy(
+                result_recv.at[0, :, :, lanes], out.at[:, 96:288, lanes], load_sem.at[block]
+            )
+        )
+        writes[-1].start()
     for block in (1, 2, 0):
         lanes = slice(128 * block, 128 * block + 128)
         for k, start in enumerate((0, 288)):
             arrived(out.at[:, start : start + 96, lanes], rest_slot + 2 * block + k)
+    for write in writes:
+        write.wait()
     for end in ends:
         end()
 
 
 def on_device(object_field, probe, amplitudes, offsets):
-    vmem = pl.BlockSpec(memory_space=pltpu.VMEM)
     left_there = pl.BlockSpec(memory_space=pl.ANY)
 
     def pair(depth):
@@ -540,7 +560,7 @@
         kernel,
         out_shape=jax.ShapeDtypeStruct((2, TILE, TILE), jnp.float32),
         in_specs=[pl.BlockSpec(memory_space=pltpu.SMEM)] + [left_there] * 5,
-        out_specs=vmem,
+        out_specs=left_there,
         scratch_shapes=[
             pltpu.VMEM((2, ROWS, COLS), jnp.float32),
             pltpu.VMEM((2, ROWS, COLS), jnp.float32),

time: 95.9 us -> 93 us (0.970)
  Pallas kernels: 93.3 us -> 90.4 us
    pallas_call x1, Pallas kernels: 93.3 us -> 90.4 us  [on_device(): pl.pallas_call(kernel, out_shape=jax.ShapeDtypeStruct((2, TILE, TILE), jn...]
where the time goes in v4:
time: 93 us; the launch traced here: 92.8 us
  Pallas kernels  90.4 us (97%)
  local copies, waits for them, and re-layouts  2.36 us (3%)
    pallas_call x1, Pallas kernels, on_device(): pl.pallas_call(kernel, out_shape=jax.ShapeDtypeStruct((2, TILE, TILE), jn...  90.4 us
    unnamed x1, local copies, waits for them, and re-layouts  2.36 us

profile of v4, /device:TPU:2, one launch (start us, length us, event | category | flops | bytes accessed | tf_op | source)
XLA Modules:
  0.0 92.8 jit_solution(3574979261638454996)
XLA Ops:
  0.0 90.4 %ptycho.1 = f32[2,384,384]{2,1,0:T(8,128)} custom-call(s32[2,2,2]{2,1,0:T(2,128)} %offsets.1, f32[2,384,384]{2,1,0:T(8,128)} %obj.1, f32[2,256,256]{2,1,0:T(8,128)} %probe_in.1, f32[512,512]{1,0:T(8,128)} %amplitudes.1, bf16[8,256,256]{2,1,0:T(8,128)(2,1)} %constant.4.clone.tables_in, bf16[2,256,256]{2,1,0:T(8,128)(2,1)} %constant.5.clone.parity_in), custom_call_target="tpu_custom_call" | custom-call | tf_op jit(solution)/shard_map/ptycho/pallas_call | solution.py:559
  90.5 2.4 %copy.8 = f32[2,384,384]{2,1,0:T(8,128)} copy(f32[2,384,384]{2,1,0:T(8,128)} %ptycho.1) | data formatting | bytes 2359296

commit v5 on v4

--- a/solution.py
+++ b/solution.py
@@ -300,7 +300,8 @@
             taker[k], near_slot + core, taker_here[k],
         )
     inner_slot = slots(2)
-    for slot, lane, width in ((far_slot, 256 * core, 128), (inner_slot, 128 - 128 * core, 256)):
+
+    def send_between(slot, lane, width):
         from_lanes = pl.ds(pl.multiple_of(lane, 128), width)
         to_lanes = pl.ds(pl.multiple_of(OWN + TILE * core + lane, 128), width)
         for k, to in enumerate((192, 0)):
@@ -309,6 +310,7 @@
                 taker[k], slot + core, taker_here[k],
             )
 
+    send_between(far_slot, 256 * core, 128)
     canvas[...] = jnp.zeros_like(canvas)
     canvas_2[...] = jnp.zeros_like(canvas_2)
     result[:, :MARGIN, :] = jnp.zeros((2, MARGIN, WIDE), jnp.float32)
@@ -328,6 +330,7 @@
                 ext.at[:, rows_from(288 - halo, 96), tile_lanes(k)], pair, pair_slot + k,
             )
         )
+    send_between(inner_slot, 128 - 128 * core, 256)
     amp_slot = slots(4)
     for j in range(2):
         for k in range(2):
@@ -450,15 +453,15 @@
     send_block(5)
     add_cols(1, canvas, grad_recv, grad_slot)
     send_block(0)
-    send_block(3)
-    send_block(4)
     next_slot = slots(2)
     for end in from_ext:
         end()
         ends.remove(end)
     take_block(1)
     take_block(2)
+    send_block(3)
     take_block(5)
+    send_block(4)
     send_cols(1, ext, own_lanes, 0, 96, next_send, next_recv, next_slot)
     take_block(0)
     send_cols(0, ext, own_lanes, 0, 96, next_send, next_recv, next_slot)

time: 93 us -> 93 us (level)
  no operation moved by 1% of the time
where the time goes in v5:
time: 93 us; the launch traced here: 92.8 us
  Pallas kernels  90.4 us (97%)
  local copies, waits for them, and re-layouts  2.36 us (3%)
    pallas_call x1, Pallas kernels, on_device(): pl.pallas_call(kernel, out_shape=jax.ShapeDtypeStruct((2, TILE, TILE), jn...  90.4 us
    unnamed x1, local copies, waits for them, and re-layouts  2.36 us

profile of v5, /device:TPU:2, one launch (start us, length us, event | category | flops | bytes accessed | tf_op | source)
XLA Modules:
  0.0 92.8 jit_solution(18389185002915552859)
XLA Ops:
  0.0 90.4 %ptycho.1 = f32[2,384,384]{2,1,0:T(8,128)} custom-call(s32[2,2,2]{2,1,0:T(2,128)} %offsets.1, f32[2,384,384]{2,1,0:T(8,128)} %obj.1, f32[2,256,256]{2,1,0:T(8,128)} %probe_in.1, f32[512,512]{1,0:T(8,128)} %amplitudes.1, bf16[8,256,256]{2,1,0:T(8,128)(2,1)} %constant.4.clone.tables_in, bf16[2,256,256]{2,1,0:T(8,128)(2,1)} %constant.5.clone.parity_in), custom_call_target="tpu_custom_call" | custom-call | tf_op jit(solution)/shard_map/ptycho/pallas_call | solution.py:562
  90.4 2.4 %copy.8 = f32[2,384,384]{2,1,0:T(8,128)} copy(f32[2,384,384]{2,1,0:T(8,128)} %ptycho.1) | data formatting | bytes 2359296
